TPU v7x, 32 devices: a whole 2x2x4 slice. The times are simulated.
32 devices in a mesh: rep: 2 (over y), seq: 8 (over z, x), head: 2 (over core).
Axes of the slice: x: 2, y: 2, z: 4, core: 2. Of those that a mesh axis runs over, the one named last changes fastest.
Arguments:
- x_in: bfloat16 [1024, 1024], P(('rep', 'seq'), 'head'), parts along dimension 0, may hold values from -6 to 6
- b_in: bfloat16 [1024, 2048], P(('rep', 'seq'), 'head'), parts along dimension 0, may hold values from -6 to 6
- c_in: bfloat16 [1024, 2048], P(('rep', 'seq'), 'head'), parts along dimension 0, may hold values from -6 to 6
- z_in: bfloat16 [1024, 1024], P(('rep', 'seq'), 'head'), parts along dimension 0, may hold values from -6 to 6
- dt_raw: bfloat16 [1024, 16], P(('rep', 'seq'), 'head'), parts along dimension 0, may hold values from -3 to 6
- dt_bias: float32 [16], P('head'), may hold values from -4 to -3
- a_log: float32 [16], P('head')
- d_skip: float32 [16], P('head'), may hold values from 0.5 to 1.5
- conv_x: bfloat16 [4, 1024], P(None, 'head'), may hold values from -3 to 3
- conv_b: bfloat16 [4, 2048], P(None, 'head'), may hold values from -3 to 3
- conv_c: bfloat16 [4, 2048], P(None, 'head'), may hold values from -3 to 3
- norm_gain: float32 [1024], P('head'), may hold values from 0.5 to 1.5
Outputs:
- mixed: bfloat16 [1024, 1024], P(('rep', 'seq'), 'head'), parts along dimension 0
There are 2 independent parts, one for each index of `rep`. A program takes and returns all parts, laid end to end along the dimension named above; an argument that names none is the same for every part. Nothing has to cross between parts.
All inputs are finite; a program needn't handle non-finite values.
Results may differ from a plain program's by a relative error of at most 0.0051.
Values may be sent and summed in bfloat16 or wider, within the bound.
No kernel may reach another device: no remote copies, remote signals or barrier semaphores. Data moves between devices by JAX's collectives and lax.ppermute only.
A program may use at most 64 MiB of HBM per device.

v0:
```python
import jax
import jax.numpy as jnp
from jax import lax
from jax.sharding import PartitionSpec as P

HEAD_DIM = 64
STATE = 256
BLOCK = 256


def causal_conv(padded, kernel, length):
    summed = jnp.zeros((length,) + padded.shape[1:], jnp.float32)
    for offset in range(kernel.shape[0]):
        summed = summed + kernel[offset].astype(jnp.float32) * padded[
            offset : offset + length
        ].astype(jnp.float32)
    return jax.nn.silu(summed).astype(jnp.bfloat16)


def blockwise_scan(x_head, b_head, c_head, rates, decays):
    length = x_head.shape[0]
    blocks = length // BLOCK
    x_part = x_head.reshape(blocks, BLOCK, -1)
    b_part = b_head.reshape(blocks, BLOCK, -1)
    c_part = c_head.reshape(blocks, BLOCK, -1)
    rate_part = rates.reshape(blocks, BLOCK)
    log_decay = jnp.cumsum(decays.reshape(blocks, BLOCK), axis=1)
    causal = jnp.arange(BLOCK)[:, None] >= jnp.arange(BLOCK)[None, :]
    scores = jnp.einsum("cin,cjn->cij", c_part, b_part, preferred_element_type=jnp.float32)
    spread = jnp.where(causal, log_decay[:, :, None] - log_decay[:, None, :], 0.0)
    mixing = jnp.where(causal, scores * jnp.exp(spread) * rate_part[:, None, :], 0.0).astype(
        jnp.bfloat16
    )
    inner = jnp.einsum("cij,cjp->cip", mixing, x_part, preferred_element_type=jnp.float32)
    weighted_b = (
        b_part.astype(jnp.float32)
        * (jnp.exp(log_decay[:, -1:] - log_decay) * rate_part)[:, :, None]
    ).astype(jnp.bfloat16)
    block_states = jnp.einsum(
        "cjn,cjp->cnp", weighted_b, x_part, preferred_element_type=jnp.float32
    )
    totals = log_decay[:, -1]

    def carry_step(state, pair):
        total, fresh = pair
        return (jnp.exp(total) * state + fresh, state)

    final_state, entering = lax.scan(
        carry_step, jnp.zeros(block_states.shape[1:], jnp.float32), (totals, block_states)
    )
    entering_low = entering.astype(jnp.bfloat16)
    outer = jnp.exp(log_decay)[:, :, None] * jnp.einsum(
        "cin,cnp->cip", c_part, entering_low, preferred_element_type=jnp.float32
    )
    return (inner + outer).reshape(length, -1)


def body(x_in, b_in, c_in, z_in, dt_raw, dt_bias, a_log, d_skip, conv_x, conv_b, conv_c, norm_gain):
    local_rows = x_in.shape[0]
    seq_total = lax.axis_size("seq")
    seq_place = lax.axis_index("seq")
    heads_here = dt_raw.shape[1]
    per_device = heads_here // seq_total
    groups_here = b_in.shape[1] // STATE
    per_group = heads_here // groups_here
    kernel_taps = conv_x.shape[0]

    def widen(groupwise, last_dim):
        row_total = groupwise.shape[0]
        copies = jnp.broadcast_to(
            groupwise.reshape(row_total, groups_here, 1, last_dim),
            (row_total, groups_here, per_group, last_dim),
        )
        return copies.reshape(row_total, seq_total, per_device, last_dim)

    x_send, b_send, c_send = (x_in, b_in, c_in)
    outgoing = (
        x_send.reshape(local_rows, seq_total, per_device, HEAD_DIM),
        widen(b_send, STATE),
        widen(c_send, STATE),
        dt_raw.reshape(local_rows, seq_total, per_device),
    )
    arrived = (
        lax.all_to_all(outgoing[0], "seq", split_axis=1, concat_axis=0, tiled=True),
        lax.all_to_all(outgoing[1], "seq", split_axis=1, concat_axis=0, tiled=True),
        lax.all_to_all(outgoing[2], "seq", split_axis=1, concat_axis=0, tiled=True),
        lax.all_to_all(outgoing[3], "seq", split_axis=1, concat_axis=0, tiled=True),
    )
    length = local_rows * seq_total
    x_heads = arrived[0].reshape(length, per_device, HEAD_DIM)
    b_heads = arrived[1].reshape(length, per_device, STATE)
    c_heads = arrived[2].reshape(length, per_device, STATE)
    raw_rates = arrived[3].reshape(length, per_device)
    kernel_x = lax.dynamic_index_in_dim(
        conv_x.reshape(kernel_taps, seq_total, per_device, HEAD_DIM), seq_place, 1, keepdims=False
    )
    kernel_b = lax.dynamic_index_in_dim(widen(conv_b, STATE), seq_place, 1, keepdims=False)
    kernel_c = lax.dynamic_index_in_dim(widen(conv_c, STATE), seq_place, 1, keepdims=False)
    front = ((kernel_taps - 1, 0), (0, 0), (0, 0))
    x_heads = causal_conv(jnp.pad(x_heads, front), kernel_x, length)
    b_heads = causal_conv(jnp.pad(b_heads, front), kernel_b, length)
    c_heads = causal_conv(jnp.pad(c_heads, front), kernel_c, length)
    first_head = seq_place * per_device
    bias_here = lax.dynamic_slice_in_dim(dt_bias, first_head, per_device)
    alog_here = lax.dynamic_slice_in_dim(a_log, first_head, per_device)
    skip_here = lax.dynamic_slice_in_dim(d_skip, first_head, per_device)
    rates = jax.nn.softplus(raw_rates.astype(jnp.float32) + bias_here[None, :])
    decays = rates * (-jnp.exp(alog_here))[None, :]
    scanned = jax.vmap(blockwise_scan, in_axes=1, out_axes=1)(
        x_heads, b_heads, c_heads, rates, decays
    )
    heads_out = (scanned + skip_here[None, :, None] * x_heads.astype(jnp.float32)).astype(
        jnp.bfloat16
    )
    returned = lax.all_to_all(
        heads_out.reshape(length, 1, per_device, HEAD_DIM),
        "seq",
        split_axis=0,
        concat_axis=1,
        tiled=True,
    )
    merged = returned.reshape(local_rows, heads_here * HEAD_DIM).astype(jnp.float32)
    gated = merged * jax.nn.silu(z_in.astype(jnp.float32))
    grouped = gated.reshape(local_rows, groups_here, -1)
    mean_square = jnp.mean(grouped * grouped, axis=-1, keepdims=True)
    normed = (grouped * lax.rsqrt(mean_square + 1e-05)).reshape(local_rows, -1)
    return (normed * norm_gain[None, :]).astype(jnp.bfloat16)


def solution(mesh):
    placed = (
        P(("rep", "seq"), "head"),
        P(("rep", "seq"), "head"),
        P(("rep", "seq"), "head"),
        P(("rep", "seq"), "head"),
        P(("rep", "seq"), "head"),
        P("head"),
        P("head"),
        P("head"),
        P(None, "head"),
        P(None, "head"),
        P(None, "head"),
        P("head"),
    )
    return jax.shard_map(
        body, mesh=mesh, in_specs=placed, out_specs=P(("rep", "seq"), "head"), check_vma=False
    )
```

profile of v0, /device:TPU:0, one launch (start us, length us, event | category | flops | bytes accessed | tf_op | source)
XLA Modules:
  0.0 69.4 jit_solution(514059991303077825)
XLA Ops:
  0.0 1.3 %copy.99 = bf16[64,8,1]{0,2,1:T(2,128)(2,1)} copy(bf16[64,8,1]{0,1,2:T(8,128)(2,1)} %bitcast.160) | data formatting | bytes 2048 | tf_op jit(solution)/shard_map/reshape | solution.py:81
  1.3 7.3 %all-to-all-start.2 = ((bf16[64,8,1]{0,2,1:T(2,128)(2,1)}), bf16[64,8,1]{0,2,1:T(2,128)(2,1)S(1)}, u32[]{:S(2)}, u32[]{:S(2)}) async-start(bf16[64,8,1]{0,2,1:T(2,128)(2,1)} %copy.99), calls=%async_computation.2 | async-start | bytes 8192 | tf_op jit(solution)/shard_map/all_to_all | solution.py:87
  8.6 0.6 copy-done.4
  9.4 0.7 copy-done.6
  10.2 0.6 copy-done.8
  10.8 0.6 dynamic_slice.30
  11.5 0.6 dynamic_slice.31
  12.8 0.8 %copy-done.3 = bf16[64,512]{1,0:T(8,128)(2,1)S(1)} copy-done((bf16[64,512]{1,0:T(8,128)(2,1)S(1)}, bf16[64,512]{1,0:T(8,128)(2,1)}, u32[]{:S(2)}) %copy-start.3) | copy-done | bytes 65560
  13.8 0.8 %reshape.665 = bf16[8,2,2048]{2,1,0:T(2,128)(2,1)} reshape(bf16[8,1,64,64]{3,2,1,0:T(8,128)(2,1)S(1)} %bitcast.145) | data formatting | bytes 131072
  14.7 0.6 copy-done.10
  15.3 0.6 dynamic_slice.33
  15.9 6.0 %all-to-all-start.3 = ((bf16[8,2,2048]{2,1,0:T(2,128)(2,1)}), bf16[8,2,2048]{2,1,0:T(2,128)(2,1)S(1)}, u32[]{:S(2)}, u32[]{:S(2)}) async-start(bf16[8,2,2048]{2,1,0:T(2,128)(2,1)} %reshape.665), calls=%async_computation.3 | async-start | bytes 131072 | tf_op jit(solution)/shard_map/all_to_all | solution.py:84
  21.9 0.6 convert_add_fusion
  22.6 0.6 reduce-window.6
  23.3 0.2 slice_reduce_fusion
  23.4 0.1 copy.118
  23.6 0.2 reduce-window.9
  24.0 4.8 %all-to-all-done.3 = bf16[8,2,2048]{2,1,0:T(2,128)(2,1)S(1)} async-done(((bf16[8,2,2048]{2,1,0:T(2,128)(2,1)}), bf16[8,2,2048]{2,1,0:T(2,128)(2,1)S(1)}, u32[]{:S(2)}, u32[]{:S(2)}) %all-to-all-start.3) | async-done | bytes 65568 | tf_op jit(solution)/shard_map/all_to_all | solution.py:84
  28.8 0.7 %broadcast_in_dim.82 = bf16[64,4,2,256]{3,0,2,1:T(8,128)(2,1)} broadcast(bf16[64,4,256]{2,0,1:T(8,128)(2,1)S(1)} %bitcast.144), dimensions={0,1,3} | broadcast | bytes 393216 | tf_op jit(solution)/shard_map/broadcast_in_dim | solution.py:70
  29.5 3.4 %all-to-all-start.1 = ((bf16[64,8,1,256]{3,0,2,1:T(8,128)(2,1)}), bf16[64,8,1,256]{3,0,2,1:T(8,128)(2,1)S(1)}, u32[]{:S(2)}, u32[]{:S(2)}) async-start(bf16[64,8,1,256]{3,0,2,1:T(8,128)(2,1)} %bitcast.12), calls=%async_computation.1 | async-start | bytes 524288 | tf_op jit(solution)/shard_map/all_to_all | solution.py:85
  33.0 0.2 reshape.666
  33.3 0.1 reshape.642
  33.4 0.2 multiply_convert_fusion.4
  33.7 7.5 %all-to-all-done.1 = bf16[64,8,1,256]{3,0,2,1:T(8,128)(2,1)S(1)} async-done(((bf16[64,8,1,256]{3,0,2,1:T(8,128)(2,1)}), bf16[64,8,1,256]{3,0,2,1:T(8,128)(2,1)S(1)}, u32[]{:S(2)}, u32[]{:S(2)}) %all-to-all-start.1) | async-done | bytes 262176 | tf_op jit(solution)/shard_map/all_to_all | solution.py:85
  41.1 0.7 %broadcast_in_dim.41 = bf16[64,4,2,256]{3,0,2,1:T(8,128)(2,1)} broadcast(bf16[64,4,256]{2,0,1:T(8,128)(2,1)S(1)} %bitcast.143), dimensions={0,1,3} | broadcast | bytes 393216 | tf_op jit(solution)/shard_map/broadcast_in_dim | solution.py:70
  41.8 3.4 %all-to-all-start = ((bf16[64,8,1,256]{3,0,2,1:T(8,128)(2,1)}), bf16[64,8,1,256]{3,0,2,1:T(8,128)(2,1)S(1)}, u32[]{:S(2)}, u32[]{:S(2)}) async-start(bf16[64,8,1,256]{3,0,2,1:T(8,128)(2,1)} %bitcast.1), calls=%async_computation | async-start | bytes 524288 | tf_op jit(solution)/shard_map/all_to_all | solution.py:86
  45.3 0.3 multiply_convert_fusion.1
  45.6 0.3 convolution_bitcast_fusion
  45.9 2.9 %while.13 = (s32[]{:T(128)}, f32[1,256,64]{2,1,0:T(8,128)S(1)}, bf16[2,1,256,64]{3,2,1,0:T(8,128)(2,1)S(1)}, f32[2,1]{0,1:T(1,128)S(1)}, f32[2,1,256,64]{2,3,0,1:T(8,128)S(1)}, /*index=5*/s32[]{:T(128)}, s32[]{:T(128)}) while((s32[]{:T(128)}, f32[1,256,64]{2,1,0:T(8,128)S(1)}, bf16[2,1,256,64]{3,2,1,0:T(8,128)(2,1)S(1)}, ...), condition=%wide.region_3.4_spmd.clone, body=%wide.region_2.3_spmd.clone.sunk | while | flops 65539 | bytes 655472 | solution.py:48
  46.1 0.6 fusion.52
  46.6 0.7 bitcast_add_fusion.4
  47.5 0.6 fusion.52
  48.1 0.7 bitcast_add_fusion.4
  48.8 4.6 %all-to-all-done = bf16[64,8,1,256]{3,0,2,1:T(8,128)(2,1)S(1)} async-done(((bf16[64,8,1,256]{3,0,2,1:T(8,128)(2,1)}), bf16[64,8,1,256]{3,0,2,1:T(8,128)(2,1)S(1)}, u32[]{:S(2)}, u32[]{:S(2)}) %all-to-all-start) | async-done | bytes 262176 | tf_op jit(solution)/shard_map/all_to_all | solution.py:86
  53.4 0.3 multiply_convert_fusion.2
  53.8 0.2 convolution_multiply_fusion.1
  54.0 0.4 fusion.4
  54.6 0.8 %fusion.22 = bf16[512,1,1,64]{0,3,2,1:T(8,128)(2,1)S(1)} fusion(f32[512,1,64]{0,2,1:T(8,128)S(1)} %reshape.647, f32[]{:T(128)} %bitcast.43, bf16[512,1,64]{0,2,1:T(8,128)(2,1)S(1)} %reshape.642, f32[64]{0:T(128)S(1)} %get-tuple-element.105, f32[64]{0:T(128)S(1)} %get-tuple-element.103, f32[64]{0:T(128)S(1)} %get-tuple-element.104, f32[64]{0:T(128)S(1)} %get-tuple-element.102), kind=kLoop, calls=%fused_computation.45 | loop fusion | flops 655360 | bytes 263172 | tf_op jit(solution)/shard_map/reshape | solution.py:116
  55.4 0.5 broadcast.205
  55.9 0.7 reduce.2
  56.7 0.2 reshape.667
  56.9 9.6 %all_to_all.63 = bf16[8,2,2048]{2,1,0:T(2,128)(2,1)S(1)} all-to-all(bf16[8,2,2048]{2,1,0:T(2,128)(2,1)S(1)} %reshape.667), channel_id=1, replica_groups=mesh['rep'=2,'seq'=8,'head'=2] {'seq'}, dimensions={0} | all-to-all | bytes 131072 | tf_op jit(solution)/shard_map/all_to_all | solution.py:115
  66.4 0.1 reshape.668
  66.8 0.2 copy.113
  67.1 0.7 %copy-done = bf16[64,512]{1,0:T(8,128)(2,1)S(1)} copy-done((bf16[64,512]{1,0:T(8,128)(2,1)S(1)}, bf16[64,512]{1,0:T(8,128)(2,1)}, u32[]{:S(2)}) %copy-start) | copy-done | bytes 65560
  67.9 0.1 reduce_sum.9
  68.2 0.5 copy-done.7
  68.8 0.7 fusion.19
  (60 shorter events, 2.2 us)
Async XLA Ops:
  1.3 14.6 %all-to-all-start.2 = ((bf16[64,8,1]{0,2,1:T(2,128)(2,1)}), bf16[64,8,1]{0,2,1:T(2,128)(2,1)S(1)}, u32[]{:S(2)}, u32[]{:S(2)}) async-start(bf16[64,8,1]{0,2,1:T(2,128)(2,1)} %copy.99), calls=%async_computation.2 | async-start | bytes 8192 | tf_op jit(solution)/shard_map/all_to_all | solution.py:87
  8.6 0.7 %copy-start.4 = (bf16[4,1024]{1,0:T(4,128)(2,1)S(1)}, bf16[4,1024]{1,0:T(4,128)(2,1)}, u32[]{:S(2)}) copy-start(bf16[4,1024]{1,0:T(4,128)(2,1)} %param.24) | copy-start | bytes 24580
  8.6 0.7 %copy-start.5 = (bf16[4,1024]{1,0:T(4,128)(2,1)S(1)}, bf16[4,1024]{1,0:T(4,128)(2,1)}, u32[]{:S(2)}) copy-start(bf16[4,1024]{1,0:T(4,128)(2,1)} %param.23) | copy-start | bytes 24580
  8.6 4.2 %copy-start.1 = (bf16[64,1024]{1,0:T(8,128)(2,1)S(1)}, bf16[64,1024]{1,0:T(8,128)(2,1)}, u32[]{:S(2)}) copy-start(bf16[64,1024]{1,0:T(8,128)(2,1)} %param.15) | copy-start | bytes 393220
  9.3 0.7 copy-start.6
  10.2 0.7 copy-start.8
  10.8 0.7 copy-start.9
  12.8 0.8 %copy-start.3 = (bf16[64,512]{1,0:T(8,128)(2,1)S(1)}, bf16[64,512]{1,0:T(8,128)(2,1)}, u32[]{:S(2)}) copy-start(bf16[64,512]{1,0:T(8,128)(2,1)} %param.14) | copy-start | bytes 196612
  13.8 0.9 %copy-start.2 = (bf16[64,1024]{1,0:T(8,128)(2,1)S(1)}, bf16[64,1024]{1,0:T(8,128)(2,1)}, u32[]{:S(2)}) copy-start(bf16[64,1024]{1,0:T(8,128)(2,1)} %param.16) | copy-start | bytes 393220
  14.7 0.7 copy-start.10
  15.9 12.9 %all-to-all-start.3 = ((bf16[8,2,2048]{2,1,0:T(2,128)(2,1)}), bf16[8,2,2048]{2,1,0:T(2,128)(2,1)S(1)}, u32[]{:S(2)}, u32[]{:S(2)}) async-start(bf16[8,2,2048]{2,1,0:T(2,128)(2,1)} %reshape.665), calls=%async_computation.3 | async-start | bytes 131072 | tf_op jit(solution)/shard_map/all_to_all | solution.py:84
  29.5 11.6 %all-to-all-start.1 = ((bf16[64,8,1,256]{3,0,2,1:T(8,128)(2,1)}), bf16[64,8,1,256]{3,0,2,1:T(8,128)(2,1)S(1)}, u32[]{:S(2)}, u32[]{:S(2)}) async-start(bf16[64,8,1,256]{3,0,2,1:T(8,128)(2,1)} %bitcast.12), calls=%async_computation.1 | async-start | bytes 524288 | tf_op jit(solution)/shard_map/all_to_all | solution.py:85
  41.8 11.6 %all-to-all-start = ((bf16[64,8,1,256]{3,0,2,1:T(8,128)(2,1)}), bf16[64,8,1,256]{3,0,2,1:T(8,128)(2,1)S(1)}, u32[]{:S(2)}, u32[]{:S(2)}) async-start(bf16[64,8,1,256]{3,0,2,1:T(8,128)(2,1)} %bitcast.1), calls=%async_computation | async-start | bytes 524288 | tf_op jit(solution)/shard_map/all_to_all | solution.py:86
  67.0 0.8 %copy-start = (bf16[64,512]{1,0:T(8,128)(2,1)S(1)}, bf16[64,512]{1,0:T(8,128)(2,1)}, u32[]{:S(2)}) copy-start(bf16[64,512]{1,0:T(8,128)(2,1)} %param.17) | copy-start | bytes 196612
  68.1 0.7 copy-start.7
where the time goes:
time: 70.2 us; the launch traced here: 69.4 us
  starting transfers between devices  20.1 us (29%)
  waiting for transfers between devices  16.9 us (24%)
  local copies, waits for them, and re-layouts  14.7 us (21%)
  blocking collectives  9.55 us (14%)
  other arithmetic  6.17 us (9%)
  between operations  1.08 us (2%)
  matrix products  0.91 us (1%)
    all_to_all x1, blocking collectives, body(): lax.all_to_all(heads_out.reshape(length, 1, per_device, HEAD_DIM), 'seq',...  9.55 us
    all_to_all x1, waiting for transfers between devices, body(): lax.all_to_all(outgoing[1], 'seq', split_axis=1, concat_axis=0, tiled=True)  7.46 us
    all_to_all x1, starting transfers between devices, body(): lax.all_to_all(outgoing[3], 'seq', split_axis=1, concat_axis=0, tiled=True)  7.28 us
    unnamed x28, local copies, waits for them, and re-layouts  6.26 us
    all_to_all x1, starting transfers between devices, body(): lax.all_to_all(outgoing[0], 'seq', split_axis=1, concat_axis=0, tiled=True)  6 us
    all_to_all x1, waiting for transfers between devices, body(): lax.all_to_all(outgoing[0], 'seq', split_axis=1, concat_axis=0, tiled=True)  4.77 us
    all_to_all x1, waiting for transfers between devices, body(): lax.all_to_all(outgoing[2], 'seq', split_axis=1, concat_axis=0, tiled=True)  4.64 us
    all_to_all x1, starting transfers between devices, body(): lax.all_to_all(outgoing[1], 'seq', split_axis=1, concat_axis=0, tiled=True)  3.41 us
  transfers between devices with their start and end apart: 4, of which 3 were waited for; matrix products, arithmetic and copies ran while one was open for 13% of the time, Pallas kernels for 0%

commit v1 on v0

--- a/solution.py
+++ b/solution.py
@@ -84,7 +84,12 @@
         lax.all_to_all(outgoing[0], "seq", split_axis=1, concat_axis=0, tiled=True),
         lax.all_to_all(outgoing[1], "seq", split_axis=1, concat_axis=0, tiled=True),
         lax.all_to_all(outgoing[2], "seq", split_axis=1, concat_axis=0, tiled=True),
-        lax.all_to_all(outgoing[3], "seq", split_axis=1, concat_axis=0, tiled=True),
+        jnp.concatenate(
+            lax.all_to_all(
+                jnp.stack(jnp.split(outgoing[3], lax.axis_size("seq"), axis=1), axis=0), "seq", 0, 0
+            ),
+            axis=0,
+        ),
     )
     length = local_rows * seq_total
     x_heads = arrived[0].reshape(length, per_device, HEAD_DIM)

time: 70.2 us -> 74.2 us (1.057)
  local copies, waits for them, and re-layouts: 14.7 us -> 19.1 us
  waiting for transfers between devices: 16.9 us -> 15.7 us
  other arithmetic: 6.17 us -> 6.93 us
    unnamed x28 -> x37, local copies, waits for them, and re-layouts: 6.26 us -> 10.8 us
    reshape x1 -> x0, local copies, waits for them, and re-layouts: 1.28 us -> none  [body(): dt_raw.reshape(local_rows, seq_total, per_device)]
    all_to_all x1, waiting for transfers between devices: 4.77 us -> 3.58 us  [body(): lax.all_to_all(outgoing[0], 'seq', split_axis=1, concat_axis=0, tiled=True)]
  transfers between devices with their start and end apart: 4 -> 4, of which waited for: 3 -> 3; matrix products, arithmetic and copies ran while one was open for 13% -> 14% of each run, Pallas kernels for 0% -> 0%
where the time goes in v1:
time: 74.2 us; the launch traced here: 73.4 us
  starting transfers between devices  20.1 us (27%)
  local copies, waits for them, and re-layouts  19.1 us (26%)
  waiting for transfers between devices  15.7 us (21%)
  blocking collectives  9.55 us (13%)
  other arithmetic  6.93 us (9%)
  between operations  1.08 us (1%)
  matrix products  0.91 us (1%)
    unnamed x37, local copies, waits for them, and re-layouts  10.8 us
    all_to_all x1, blocking collectives, body(): lax.all_to_all(heads_out.reshape(length, 1, per_device, HEAD_DIM), 'seq',...  9.55 us
    all_to_all x1, waiting for transfers between devices, body(): lax.all_to_all(outgoing[1], 'seq', split_axis=1, concat_axis=0, tiled=True)  7.46 us
    all_to_all x1, starting transfers between devices, body(): lax.all_to_all(jnp.stack(jnp.split(outgoing[3], lax.axis_size('seq'), axi...  7.28 us
    all_to_all x1, starting transfers between devices, body(): lax.all_to_all(outgoing[0], 'seq', split_axis=1, concat_axis=0, tiled=True)  6 us
    all_to_all x1, waiting for transfers between devices, body(): lax.all_to_all(outgoing[2], 'seq', split_axis=1, concat_axis=0, tiled=True)  4.64 us
    all_to_all x1, waiting for transfers between devices, body(): lax.all_to_all(outgoing[0], 'seq', split_axis=1, concat_axis=0, tiled=True)  3.58 us
    all_to_all x1, starting transfers between devices, body(): lax.all_to_all(outgoing[1], 'seq', split_axis=1, concat_axis=0, tiled=True)  3.41 us
  transfers between devices with their start and end apart: 4, of which 3 were waited for; matrix products, arithmetic and copies ran while one was open for 14% of the time, Pallas kernels for 0%

profile of v1, /device:TPU:0, one launch (start us, length us, event | category | flops | bytes accessed | tf_op | source)
XLA Modules:
  0.0 73.4 jit_solution(9491784711515979295)
XLA Ops:
  0.0 1.3 %constant_dynamic-update-slice_fusion.7 = bf16[8,64,1,1]{1,3,2,0:T(2,128)(2,1)} fusion(bf16[64,8,1]{0,1,2:T(8,128)(2,1)} %bitcast.166), kind=kLoop, calls=%fused_computation.56 | loop fusion | bytes 640
  1.3 0.5 constant_dynamic-update-slice_fusion.6
  1.8 0.5 constant_dynamic-update-slice_fusion.5
  2.4 0.5 constant_dynamic-update-slice_fusion.4
  2.9 0.5 constant_dynamic-update-slice_fusion.3
  3.4 0.5 constant_dynamic-update-slice_fusion.2
  4.0 0.6 constant_dynamic-update-slice_fusion.1
  4.5 0.5 constant_dynamic-update-slice_fusion
  5.0 7.3 %all-to-all-start.2 = ((bf16[8,64,1,1]{1,3,2,0:T(2,128)(2,1)}), bf16[8,64,1,1]{1,3,2,0:T(2,128)(2,1)S(1)}, u32[]{:S(2)}, u32[]{:S(2)}) async-start(bf16[8,64,1,1]{1,3,2,0:T(2,128)(2,1)} %constant_dynamic-update-slice_fusion), calls=%async_computation.2 | async-start | bytes 8192 | tf_op jit(solution)/shard_map/all_to_all | solution.py:88
  12.4 0.6 copy-done.4
  13.1 0.7 copy-done.6
  14.0 0.6 copy-done.9
  14.6 0.6 dynamic_slice.30
  15.3 0.6 dynamic_slice.31
  16.6 0.8 %copy-done.3 = bf16[64,512]{1,0:T(8,128)(2,1)S(1)} copy-done((bf16[64,512]{1,0:T(8,128)(2,1)S(1)}, bf16[64,512]{1,0:T(8,128)(2,1)}, u32[]{:S(2)}) %copy-start.3) | copy-done | bytes 65560
  17.5 0.8 %reshape.669 = bf16[8,2,2048]{2,1,0:T(2,128)(2,1)} reshape(bf16[8,1,64,64]{3,2,1,0:T(8,128)(2,1)S(1)} %bitcast.152) | data formatting | bytes 131072
  18.4 0.6 copy-done.11
  19.1 0.7 dynamic_slice.33
  19.7 6.0 %all-to-all-start.3 = ((bf16[8,2,2048]{2,1,0:T(2,128)(2,1)}), bf16[8,2,2048]{2,1,0:T(2,128)(2,1)S(1)}, u32[]{:S(2)}, u32[]{:S(2)}) async-start(bf16[8,2,2048]{2,1,0:T(2,128)(2,1)} %reshape.669), calls=%async_computation.3 | async-start | bytes 131072 | tf_op jit(solution)/shard_map/all_to_all | solution.py:84
  25.7 0.6 broadcast.202
  26.3 1.3 %fusion.47 = (f32[8,64]{1,0:T(8,128)S(1)}, f32[8,64,1,1]{1,3,2,0:T(1,128)S(1)}) fusion(f32[]{:T(128)} %broadcast.202, f32[]{:T(128)} %bitcast.31, bf16[8,64,1,1]{1,3,2,0:T(2,128)(2,1)S(1)} %all-to-all-done.2), kind=kLoop, calls=%fused_computation.99 | loop fusion | flops 1024 | bytes 5128 | tf_op jit(solution)/shard_map/add | solution.py:112
  27.7 0.6 reduce-window.6
  28.6 0.2 reduce-window.9
  29.1 3.6 %all-to-all-done.3 = bf16[8,2,2048]{2,1,0:T(2,128)(2,1)S(1)} async-done(((bf16[8,2,2048]{2,1,0:T(2,128)(2,1)}), bf16[8,2,2048]{2,1,0:T(2,128)(2,1)S(1)}, u32[]{:S(2)}, u32[]{:S(2)}) %all-to-all-start.3) | async-done | bytes 65568 | tf_op jit(solution)/shard_map/all_to_all | solution.py:84
  32.7 0.7 broadcast_in_dim.82
  33.4 3.4 %all-to-all-start.1 = ((bf16[64,8,1,256]{3,0,2,1:T(8,128)(2,1)}), bf16[64,8,1,256]{3,0,2,1:T(8,128)(2,1)S(1)}, u32[]{:S(2)}, u32[]{:S(2)}) async-start(bf16[64,8,1,256]{3,0,2,1:T(8,128)(2,1)} %bitcast.12), calls=%async_computation.1 | async-start | bytes 524288 | tf_op jit(solution)/shard_map/all_to_all | solution.py:85
  37.3 0.2 multiply_convert_fusion.4
  37.5 7.5 %all-to-all-done.1 = bf16[64,8,1,256]{3,0,2,1:T(8,128)(2,1)S(1)} async-done(((bf16[64,8,1,256]{3,0,2,1:T(8,128)(2,1)}), bf16[64,8,1,256]{3,0,2,1:T(8,128)(2,1)S(1)}, u32[]{:S(2)}, u32[]{:S(2)}) %all-to-all-start.1) | async-done | bytes 262176 | tf_op jit(solution)/shard_map/all_to_all | solution.py:85
  44.9 0.7 broadcast_in_dim.41
  45.7 3.4 %all-to-all-start = ((bf16[64,8,1,256]{3,0,2,1:T(8,128)(2,1)}), bf16[64,8,1,256]{3,0,2,1:T(8,128)(2,1)S(1)}, u32[]{:S(2)}, u32[]{:S(2)}) async-start(bf16[64,8,1,256]{3,0,2,1:T(8,128)(2,1)} %bitcast.1), calls=%async_computation | async-start | bytes 524288 | tf_op jit(solution)/shard_map/all_to_all | solution.py:86
  49.1 0.3 multiply_convert_fusion.1
  49.4 0.3 convolution_bitcast_fusion
  49.7 2.9 %while.13 = (s32[]{:T(128)}, f32[1,256,64]{2,1,0:T(8,128)S(1)}, bf16[2,1,256,64]{3,2,1,0:T(8,128)(2,1)S(1)}, f32[2,1]{0,1:T(1,128)S(1)}, f32[2,1,256,64]{2,3,0,1:T(8,128)S(1)}, /*index=5*/s32[]{:T(128)}, s32[]{:T(128)}) while((s32[]{:T(128)}, f32[1,256,64]{2,1,0:T(8,128)S(1)}, bf16[2,1,256,64]{3,2,1,0:T(8,128)(2,1)S(1)}, ...), condition=%wide.region_3.4_spmd.clone, body=%wide.region_2.3_spmd.clone.sunk | while | flops 65539 | bytes 655472 | solution.py:48
  49.9 0.6 fusion.53
  50.5 0.7 bitcast_add_fusion.4
  51.3 0.6 fusion.53
  51.9 0.7 bitcast_add_fusion.4
  52.6 4.6 %all-to-all-done = bf16[64,8,1,256]{3,0,2,1:T(8,128)(2,1)S(1)} async-done(((bf16[64,8,1,256]{3,0,2,1:T(8,128)(2,1)}), bf16[64,8,1,256]{3,0,2,1:T(8,128)(2,1)S(1)}, u32[]{:S(2)}, u32[]{:S(2)}) %all-to-all-start) | async-done | bytes 262176 | tf_op jit(solution)/shard_map/all_to_all | solution.py:86
  57.2 0.3 multiply_convert_fusion.2
  57.6 0.2 convolution_multiply_fusion.1
  57.8 0.4 fusion.4
  58.4 0.9 %fusion.22 = bf16[512,1,1,64]{0,3,2,1:T(8,128)(2,1)S(1)} fusion(f32[512,1,64]{0,2,1:T(8,128)S(1)} %reshape.639, f32[]{:T(128)} %bitcast.48, bf16[512,1,64]{0,2,1:T(8,128)(2,1)S(1)} %reshape.634, f32[64]{0:T(128)S(1)} %get-tuple-element.102, f32[64]{0:T(128)S(1)} %get-tuple-element.100, f32[64]{0:T(128)S(1)} %get-tuple-element.101, f32[64]{0:T(128)S(1)} %get-tuple-element.99), kind=kLoop, calls=%fused_computation.45 | loop fusion | flops 655360 | bytes 263172 | tf_op jit(solution)/shard_map/reshape | solution.py:121
  59.3 0.5 broadcast.203
  59.8 0.7 reduce.9
  60.8 9.6 %all_to_all.59 = bf16[8,2,2048]{2,1,0:T(2,128)(2,1)S(1)} all-to-all(bf16[8,2,2048]{2,1,0:T(2,128)(2,1)S(1)} %reshape.671), channel_id=1, replica_groups=mesh['rep'=2,'seq'=8,'head'=2] {'seq'}, dimensions={0} | all-to-all | bytes 131072 | tf_op jit(solution)/shard_map/all_to_all | solution.py:120
  71.0 0.7 copy-done
  72.2 0.5 copy-done.7
  72.7 0.7 fusion.19
  (70 shorter events, 3.5 us)
Async XLA Ops:
  0.0 1.3 %copy-start.8 = (bf16[64,8]{0,1:T(8,128)(2,1)S(1)}, bf16[64,8]{0,1:T(8,128)(2,1)}, u32[]{:S(2)}) copy-start(bf16[64,8]{0,1:T(8,128)(2,1)} %param.18) | copy-start | bytes 3076
  5.0 14.7 %all-to-all-start.2 = ((bf16[8,64,1,1]{1,3,2,0:T(2,128)(2,1)}), bf16[8,64,1,1]{1,3,2,0:T(2,128)(2,1)S(1)}, u32[]{:S(2)}, u32[]{:S(2)}) async-start(bf16[8,64,1,1]{1,3,2,0:T(2,128)(2,1)} %constant_dynamic-update-slice_fusion), calls=%async_computation.2 | async-start | bytes 8192 | tf_op jit(solution)/shard_map/all_to_all | solution.py:88
  12.3 0.7 copy-start.4
  12.3 0.7 %copy-start.5 = (bf16[4,1024]{1,0:T(4,128)(2,1)S(1)}, bf16[4,1024]{1,0:T(4,128)(2,1)}, u32[]{:S(2)}) copy-start(bf16[4,1024]{1,0:T(4,128)(2,1)} %param.23) | copy-start | bytes 24580
  12.4 4.2 %copy-start.1 = (bf16[64,1024]{1,0:T(8,128)(2,1)S(1)}, bf16[64,1024]{1,0:T(8,128)(2,1)}, u32[]{:S(2)}) copy-start(bf16[64,1024]{1,0:T(8,128)(2,1)} %param.15) | copy-start | bytes 393220
  13.1 0.7 copy-start.6
  13.9 0.7 copy-start.9
  14.6 0.7 copy-start.10
  16.5 0.8 %copy-start.3 = (bf16[64,512]{1,0:T(8,128)(2,1)S(1)}, bf16[64,512]{1,0:T(8,128)(2,1)}, u32[]{:S(2)}) copy-start(bf16[64,512]{1,0:T(8,128)(2,1)} %param.14) | copy-start | bytes 196612
  17.5 0.9 %copy-start.2 = (bf16[64,1024]{1,0:T(8,128)(2,1)S(1)}, bf16[64,1024]{1,0:T(8,128)(2,1)}, u32[]{:S(2)}) copy-start(bf16[64,1024]{1,0:T(8,128)(2,1)} %param.16) | copy-start | bytes 393220
  18.4 0.7 copy-start.11
  19.7 12.9 %all-to-all-start.3 = ((bf16[8,2,2048]{2,1,0:T(2,128)(2,1)}), bf16[8,2,2048]{2,1,0:T(2,128)(2,1)S(1)}, u32[]{:S(2)}, u32[]{:S(2)}) async-start(bf16[8,2,2048]{2,1,0:T(2,128)(2,1)} %reshape.669), calls=%async_computation.3 | async-start | bytes 131072 | tf_op jit(solution)/shard_map/all_to_all | solution.py:84
  33.4 11.6 %all-to-all-start.1 = ((bf16[64,8,1,256]{3,0,2,1:T(8,128)(2,1)}), bf16[64,8,1,256]{3,0,2,1:T(8,128)(2,1)S(1)}, u32[]{:S(2)}, u32[]{:S(2)}) async-start(bf16[64,8,1,256]{3,0,2,1:T(8,128)(2,1)} %bitcast.12), calls=%async_computation.1 | async-start | bytes 524288 | tf_op jit(solution)/shard_map/all_to_all | solution.py:85
  45.7 11.6 %all-to-all-start = ((bf16[64,8,1,256]{3,0,2,1:T(8,128)(2,1)}), bf16[64,8,1,256]{3,0,2,1:T(8,128)(2,1)S(1)}, u32[]{:S(2)}, u32[]{:S(2)}) async-start(bf16[64,8,1,256]{3,0,2,1:T(8,128)(2,1)} %bitcast.1), calls=%async_computation | async-start | bytes 524288 | tf_op jit(solution)/shard_map/all_to_all | solution.py:86
  70.9 0.8 %copy-start = (bf16[64,512]{1,0:T(8,128)(2,1)S(1)}, bf16[64,512]{1,0:T(8,128)(2,1)}, u32[]{:S(2)}) copy-start(bf16[64,512]{1,0:T(8,128)(2,1)} %param.17) | copy-start | bytes 196612
  72.0 0.7 copy-start.7
